TPU v7x, 32 devices: a whole 2x2x4 slice. The times are simulated.
32 devices in a mesh: pb: 2 (over core), ka: 16 (over z, y, x).
Axes of the slice: x: 2, y: 2, z: 4, core: 2. Of those that a mesh axis runs over, the one named last changes fastest.
Arguments:
- vertex_ladder: float32 [2, 8, 1024, 1024], P(None, 'pb', 'ka'), may hold values from -6 to 6
- vertex_cross_a: float32 [2, 8, 1024, 1024], P(None, 'pb', 'ka'), may hold values from -6 to 6
- vertex_cross_b: float32 [2, 8, 1024, 1024], P(None, 'pb', 'ka'), may hold values from -6 to 6
- bubble: float32 [2, 8, 1024], P(None, 'pb'), may hold values from -0.072 to 0.072
- row_maps: int32 [2, 8, 1024], replicated, may hold values from 0 to 8191, as said below
- col_maps: int32 [2, 1024], replicated, may hold values from 0 to 1023, each once within a row
Outputs:
- ladder_out: float32 [2, 8, 1024, 1024], P(None, 'pb', 'ka')
- crossed_a: float32 [2, 8, 1024, 1024], P(None, 'pb', 'ka')
- crossed_b: float32 [2, 8, 1024, 1024], P(None, 'pb', 'ka')
Inputs may be any that keep to these rules, and one draw needn't show every extreme that they name: `row_maps`: each of the two maps is a permutation of all 8192 rows. A device holds the rows of its bosonic indices (index of pb) and its first fermionic indices (index of ka); the 256 rows of one device take exactly 8 of their source rows from each device.
All inputs are finite; a program needn't handle non-finite values.
Results may differ from a plain program's by a relative error of at most 0.007.
Values may be sent and summed in bfloat16 or wider, within the bound.
No kernel may reach another device: no remote copies, remote signals or barrier semaphores. Data moves between devices by JAX's collectives and lax.ppermute only.
A program may use at most 64 MiB of HBM per device.

v0:
```python
import jax
import jax.numpy as jnp
from jax import lax
from jax.sharding import PartitionSpec as P

LADDER = 6


def ladder_rows(vertex_rows, bubble_q, gathered):
    col_count = gathered.shape[2]
    row_count = vertex_rows.shape[1]
    right_op = jnp.concatenate([gathered[0], gathered[1]], 1)
    current = vertex_rows
    for _ in range(LADDER):
        scaled_re = current[0] * bubble_q[0][None, :] - current[1] * bubble_q[1][None, :]
        scaled_im = current[0] * bubble_q[1][None, :] + current[1] * bubble_q[0][None, :]
        left_op = jnp.concatenate([scaled_re, scaled_im], 0).astype(jnp.bfloat16)
        product = jnp.dot(left_op, right_op, preferred_element_type=jnp.float32)
        real_part = product[:row_count, :col_count] - product[row_count:, col_count:]
        imag_part = product[:row_count, col_count:] + product[row_count:, :col_count]
        current = vertex_rows + jnp.stack([real_part, imag_part])
    return current


def per_device(vertex_ladder, vertex_cross_a, vertex_cross_b, bubble, row_maps, col_maps):
    q_local = vertex_ladder.shape[1]
    row_count = vertex_ladder.shape[2]
    col_count = vertex_ladder.shape[3]
    gamma_low = vertex_ladder.astype(jnp.bfloat16)
    whole_low = lax.all_gather(gamma_low, "ka", axis=2, tiled=True)

    def per_whole(loop_state, scan_items):
        vertex_rows, gathered, bubble_q = scan_items
        return (loop_state, ladder_rows(vertex_rows, bubble_q, gathered))

    _, stacked = lax.scan(
        per_whole,
        jnp.int32(0),
        (
            jnp.moveaxis(vertex_ladder, 1, 0),
            jnp.moveaxis(whole_low, 1, 0),
            jnp.moveaxis(bubble, 1, 0),
        ),
    )
    ladder_out = jnp.moveaxis(stacked, 0, 1)
    local_count = q_local * row_count
    reducible = (ladder_out - vertex_ladder).reshape(2, local_count, col_count)
    pb_count = lax.axis_size("pb")
    ka_count = lax.axis_size("ka")
    dev_count = pb_count * ka_count
    per_peer = local_count // dev_count
    my_device = lax.axis_index("pb") * ka_count + lax.axis_index("ka")
    my_bos = lax.axis_index("pb") * q_local + jnp.arange(q_local, dtype=jnp.int32)
    my_fer = lax.axis_index("ka") * row_count + jnp.arange(row_count, dtype=jnp.int32)
    my_rows = (my_bos[:, None] * col_count + my_fer[None, :]).reshape(-1)
    slot_ids = jnp.arange(per_peer, dtype=jnp.int32)

    def device_of(global_rows):
        return global_rows // col_count // q_local * ka_count + global_rows % col_count // row_count

    def prepare(table_flat):
        by_device = (
            table_flat.reshape(pb_count, q_local, ka_count, row_count)
            .transpose(0, 2, 1, 3)
            .reshape(dev_count, local_count)
        )
        mine = (device_of(by_device) == my_device).astype(jnp.int32)
        rank = jnp.cumsum(mine, 1) - 1
        source_local = (
            by_device // col_count % q_local * row_count + by_device % col_count % row_count
        )
        hits = mine[:, :, None] * (rank[:, :, None] == slot_ids[None, None, :]).astype(jnp.int32)
        send_index = jnp.sum(hits * source_local[:, :, None], 1).reshape(-1)
        return jnp.take(reducible, send_index, axis=1)

    def place(table_flat, received, column_map):
        source = table_flat[my_rows]
        source_dev = device_of(source)
        onehot = (source_dev[:, None] == jnp.arange(dev_count, dtype=jnp.int32)[None, :]).astype(
            jnp.int32
        )
        slot_index = jnp.sum((jnp.cumsum(onehot, 0) - onehot) * onehot, 1)
        picked = jnp.take(received, source_dev * per_peer + slot_index, axis=1)
        selector = (jnp.arange(col_count, dtype=jnp.int32)[:, None] == column_map[None, :]).astype(
            jnp.float32
        )
        picked = jnp.einsum("prk,km->prm", picked, selector, precision=lax.Precision.HIGHEST)
        return picked.reshape(2, q_local, row_count, col_count)

    table_a = row_maps[0].reshape(-1)
    table_b = row_maps[1].reshape(-1)
    send_a = prepare(table_a)
    send_b = prepare(table_b)
    recv_a, recv_b = (
        lax.all_to_all(send_a, ("pb", "ka"), split_axis=1, concat_axis=1, tiled=True),
        lax.all_to_all(send_b, ("pb", "ka"), split_axis=1, concat_axis=1, tiled=True),
    )
    crossed_a = vertex_cross_a + place(table_a, recv_a, col_maps[0])
    crossed_b = vertex_cross_b + place(table_b, recv_b, col_maps[1])
    return (ladder_out, crossed_a, crossed_b)


def solution(mesh):
    return jax.shard_map(
        per_device,
        mesh=mesh,
        in_specs=(
            P(None, "pb", "ka", None),
            P(None, "pb", "ka", None),
            P(None, "pb", "ka", None),
            P(None, "pb", None),
            P(),
            P(),
        ),
        out_specs=(P(None, "pb", "ka", None), P(None, "pb", "ka", None), P(None, "pb", "ka", None)),
        check_vma=False,
    )
```

profile of v0, /device:TPU:0, one launch (start us, length us, event | category | flops | bytes accessed | tf_op | source)
XLA Modules:
  0.0 381.2 jit_solution(11262854710997987744)
XLA Ops:
  7.2 2.7 copy.84
  10.0 1.8 copy.85
  14.5 190.7 %all-gather.2.cloned.1.call-done = bf16[2,4,1024,1024]{3,2,0,1:T(8,128)(2,1)} async-done(((bf16[2,4,64,1024]{3,2,0,1:T(8,128)(2,1)}), bf16[2,4,1024,1024]{3,2,0,1:T(8,128)(2,1)}) %all-gather.2.cloned.1.call-update) | async-done | bytes 16777232 | tf_op jit(solution)/shard_map/all_gather | solution.py:30
  205.2 37.3 %while.10 = (s32[]{:T(128)}, f32[4,2,64,1024]{3,2,0,1:T(8,128)}, f32[4,2,64,1024]{3,2,1,0:T(8,128)S(1)}, f32[4,2,1024]{2,1,0:T(2,128)S(1)}, bf16[4,2,1024,1024]{...) while((s32[]{:T(128)}, f32[4,2,64,1024]{3,2,0,1:T(8,128)}, f32[4,2,64,1024]{3,2,1,0:T(8,128)S(1)}, ...), condition=%wide.region_1.2_spmd, body=%wide.region_0.1_spmd.sunk | while | flops 3280207872 | bytes 65077400 | solution.py:36
  205.3 2.7 dynamic-slice_bitcast_fusion.5
  214.6 2.7 dynamic-slice_bitcast_fusion.5
  223.9 2.7 dynamic-slice_bitcast_fusion.5
  233.2 2.7 dynamic-slice_bitcast_fusion.5
  242.4 2.6 bitcast_subtract_fusion
  246.7 4.0 %gather_fusion.2 = f32[256,2,1024]{2,1,0:T(2,128)} fusion(f32[2,256,1024]{2,0,1:T(2,128)S(1)} %bitcast.287, s32[1024]{0:T(1024)S(1)} %pad_clamp_fusion.3), kind=kCustom, calls=%fused_computation.clone | custom fusion | bytes 4195328 | tf_op jit(solution)/shard_map/jit(_take)/gather | solution.py:74
  250.7 3.6 select_bitcast_fusion.3
  254.3 3.7 all-to-all-start
  259.7 4.0 %gather_fusion.4 = f32[256,2,1024]{2,1,0:T(2,128)} fusion(f32[2,256,1024]{2,0,1:T(2,128)S(1)} %bitcast.288, s32[1024]{0:T(1024)S(1)} %pad_clamp_fusion.1), kind=kCustom, calls=%fused_computation.2.clone | custom fusion | bytes 4195328 | tf_op jit(solution)/shard_map/jit(_take)/gather | solution.py:74
  263.7 3.6 select_bitcast_fusion.1
  267.3 41.0 %all-to-all-done = f32[2,256,1024]{2,0,1:T(2,128)} async-done(((f32[2,256,1024]{2,0,1:T(2,128)}), f32[2,256,1024]{2,0,1:T(2,128)}, u32[]{:S(2)}, u32[]{:S(2)}) %all-to-all-start) | async-done | bytes 2097184 | tf_op jit(solution)/shard_map/all_to_all | solution.py:95
  308.3 2.7 all-to-all-start.1
  313.9 1.7 gather_fusion.1
  316.8 5.6 %gather_fusion.3 = f32[256,2,1024]{2,1,0:T(2,128)} fusion(f32[2,256,1024]{2,0,1:T(2,128)} %all-to-all-done, s32[1024]{0:T(1024)S(1)} %pad_clamp_fusion.2), kind=kCustom, calls=%fused_computation.1.clone | custom fusion | bytes 4195328 | tf_op jit(solution)/shard_map/jit(_take)/gather | solution.py:83
  322.5 2.6 select_bitcast_fusion.2
  325.1 4.0 %fusion.45 = f32[2,256,1024]{2,1,0:T(8,128)S(1)} fusion(f32[2,256,1024]{2,0,1:T(2,128)S(1)} %select_bitcast_fusion.2, s32[1024]{0:T(1024)S(1)} %bitcast.311), kind=kOutput, calls=%fused_computation.100 | convolution fusion | flops 6443499520 | bytes 4198400 | tf_op jit(solution)/shard_map/prk,km->prm/dot_general | solution.py:87
  330.9 30.8 %all-to-all-done.1 = f32[2,256,1024]{2,0,1:T(2,128)S(1)} async-done(((f32[2,256,1024]{2,0,1:T(2,128)}), f32[2,256,1024]{2,0,1:T(2,128)S(1)}, u32[]{:S(2)}, u32[]{:S(2)}) %all-to-all-start.1) | async-done | bytes 2097184 | tf_op jit(solution)/shard_map/all_to_all | solution.py:96
  361.7 4.0 %gather_fusion.5 = f32[256,2,1024]{2,1,0:T(2,128)} fusion(f32[2,256,1024]{2,0,1:T(2,128)S(1)} %all-to-all-done.1, s32[1024]{0:T(1024)S(1)} %pad_clamp_fusion), kind=kCustom, calls=%fused_computation.3.clone | custom fusion | bytes 4195328 | tf_op jit(solution)/shard_map/jit(_take)/gather | solution.py:83
  365.7 2.9 select_bitcast_fusion
  368.6 4.0 %fusion.48 = f32[2,256,1024]{2,1,0:T(8,128)S(1)} fusion(f32[2,256,1024]{2,0,1:T(2,128)S(1)} %select_bitcast_fusion, s32[1024]{0:T(1024)S(1)} %bitcast.310), kind=kOutput, calls=%fused_computation.102 | convolution fusion | flops 6443499520 | bytes 4198400 | tf_op jit(solution)/shard_map/prk,km->prm/dot_general | solution.py:87
  (179 shorter events, 39.4 us)
Async XLA Ops:
  7.2 198.0 %all-gather.2.cloned.1.call-start = ((), (), s32[]{:S(2)}) async-start(), calls=%async_computation.2 | async-start | bytes 17825792 | tf_op jit(solution)/shard_map/all_gather | solution.py:30
  10.0 1.8 copy-start.2
  10.0 2.4 copy-start.3
  254.3 54.1 %all-to-all-start = ((f32[2,256,1024]{2,0,1:T(2,128)}), f32[2,256,1024]{2,0,1:T(2,128)}, u32[]{:S(2)}, u32[]{:S(2)}) async-start(f32[2,256,1024]{2,0,1:T(2,128)} %select_bitcast_fusion.3), calls=%async_computation | async-start | bytes 4194304 | tf_op jit(solution)/shard_map/all_to_all | solution.py:95
  308.3 53.3 %all-to-all-start.1 = ((f32[2,256,1024]{2,0,1:T(2,128)}), f32[2,256,1024]{2,0,1:T(2,128)S(1)}, u32[]{:S(2)}, u32[]{:S(2)}) async-start(f32[2,256,1024]{2,0,1:T(2,128)} %select_bitcast_fusion.1), calls=%async_computation.1 | async-start | bytes 4194304 | tf_op jit(solution)/shard_map/all_to_all | solution.py:96
  311.1 5.7 %copy-start.4 = (s32[2,1024]{1,0:T(2,128)S(1)}, s32[2,1024]{1,0:T(2,128)}, u32[]{:S(2)}) copy-start(s32[2,1024]{1,0:T(2,128)} %param.15) | copy-start | bytes 24580
  325.1 4.0 %copy-start = (f32[2,4,64,1024]{3,2,1,0:T(8,128)S(1)}, f32[2,4,64,1024]{3,2,1,0:T(8,128)}, u32[]{:S(2)}) copy-start(f32[2,4,64,1024]{3,2,1,0:T(8,128)} %param.11) | copy-start | bytes 6291460
  368.6 4.0 %copy-start.1 = (f32[2,4,64,1024]{3,2,1,0:T(8,128)S(1)}, f32[2,4,64,1024]{3,2,1,0:T(8,128)}, u32[]{:S(2)}) copy-start(f32[2,4,64,1024]{3,2,1,0:T(8,128)} %param.12) | copy-start | bytes 6291460
Sparse Core Ops, SparseCore 0:
  11.3 193.8 all-gather.1
where the time goes:
time: 382 us; the launch traced here: 381 us
  waiting for transfers between devices  262 us (69%)
  local copies, waits for them, and re-layouts  39.7 us (10%)
  other arithmetic  32 us (8%)
  matrix products  25.6 us (7%)
  between operations  14.4 us (4%)
  starting transfers between devices  6.42 us (2%)
    all_gather x1, waiting for transfers between devices, per_device(): whole_low = lax.all_gather(gamma_low, 'ka', axis=2, tiled=True)  191 us
    all_to_all x1, waiting for transfers between devices, per_device(): lax.all_to_all(send_a, ('pb', 'ka'), split_axis=1, concat_axis=1, tiled=T...  41 us
    all_to_all x1, waiting for transfers between devices, per_device(): lax.all_to_all(send_b, ('pb', 'ka'), split_axis=1, concat_axis=1, tiled=T...  30.8 us
    dot_general x24, matrix products, ladder_rows(): product = jnp.dot(left_op, right_op, preferred_element_type=jnp.float32)  17.6 us
    squeeze x4, local copies, waits for them, and re-layouts, ladder_rows(): right_op = jnp.concatenate([gathered[0], gathered[1]], 1)  10.7 us
    gather x2, local copies, waits for them, and re-layouts, place(): picked = jnp.take(received, source_dev * per_peer + slot_index, axis=1)  9.65 us
    gather x2, local copies, waits for them, and re-layouts, prepare(): return jnp.take(reducible, send_index, axis=1)  8.05 us
    dot_general x2, matrix products, place(): jnp.einsum('prk,km->prm', picked, selector, precision=lax.Precision.HIGHEST)  8.03 us
  transfers between devices with their start and end apart: 3, of which 3 were waited for; matrix products, arithmetic and copies ran while one was open for 9% of the time, Pallas kernels for 0%

commit v1 on v0

--- a/solution.py
+++ b/solution.py
@@ -4,6 +4,28 @@
 from jax.sharding import PartitionSpec as P
 
 LADDER = 6
+
+
+def in_order(blocks, dim):
+    shape = list(blocks.shape[1:])
+    shape[dim] *= blocks.shape[0]
+    return jnp.moveaxis(blocks, 0, dim).reshape(shape)
+
+
+def gather_around(x, axis, dim):
+    devices = lax.axis_size(axis)
+    pairs = [(i, (i + 1) % devices) for i in range(devices)]
+    back = [(b, a) for a, b in pairs]
+    lower, upper = ([], [])
+    for step in range(devices - 1):
+        if step % 2 == 0:
+            lower.append(lax.ppermute(lower[-1] if lower else x, axis, pairs))
+        else:
+            upper.append(lax.ppermute(upper[-1] if upper else x, axis, back))
+    parts = jnp.stack([*lower[::-1], x, *upper])
+    shift = lax.axis_index(axis) - len(lower)
+    parts = parts[(jnp.arange(devices) - shift) % devices]
+    return in_order(parts, dim)
 
 
 def ladder_rows(vertex_rows, bubble_q, gathered):
@@ -27,7 +49,7 @@
     row_count = vertex_ladder.shape[2]
     col_count = vertex_ladder.shape[3]
     gamma_low = vertex_ladder.astype(jnp.bfloat16)
-    whole_low = lax.all_gather(gamma_low, "ka", axis=2, tiled=True)
+    whole_low = gather_around(gamma_low, "ka", 2)
 
     def per_whole(loop_state, scan_items):
         vertex_rows, gathered, bubble_q = scan_items

time: 382 us -> 597 us (1.56)
  starting transfers between devices: 6.42 us -> 172 us
  local copies, waits for them, and re-layouts: 39.7 us -> 89.9 us
  between operations: 14.4 us -> 1.34 us
    ppermute x0 -> x15, waiting for transfers between devices: none -> 194 us  [the longest x8 190 us: gather_around(): lower.append(lax.ppermute(lower[-1] if lower else x, axis, pairs))]
    all_gather x1 -> x0, waiting for transfers between devices: 191 us -> none  [per_device(): whole_low = lax.all_gather(gamma_low, 'ka', axis=2, tiled=True)]
    ppermute x0 -> x15, starting transfers between devices: none -> 149 us  [the longest x7 108 us: gather_around(): upper.append(lax.ppermute(upper[-1] if upper else x, axis, back))]
    unnamed x14 -> x61, local copies, waits for them, and re-layouts: 4.56 us -> 26.2 us
    all_to_all x1, starting transfers between devices: 2.73 us -> 20.6 us  [per_device(): lax.all_to_all(send_b, ('pb', 'ka'), split_axis=1, concat_axis=1, tiled=T...]
    transpose x0 -> x1, local copies, waits for them, and re-layouts: none -> 14.1 us  [in_order(): return jnp.moveaxis(blocks, 0, dim).reshape(shape)]
    gather x0 -> x1, local copies, waits for them, and re-layouts: none -> 13.4 us  [gather_around(): parts = parts[(jnp.arange(devices) - shift) % devices]]
    all_to_all x1, waiting for transfers between devices: 30.8 us -> 42.7 us  [per_device(): lax.all_to_all(send_b, ('pb', 'ka'), split_axis=1, concat_axis=1, tiled=T...]
  transfers between devices with their start and end apart: 3 -> 17, of which waited for: 3 -> 12; matrix products, arithmetic and copies ran while one was open for 9% -> 10% of each run, Pallas kernels for 0% -> 0%
where the time goes in v1:
time: 597 us; the launch traced here: 592 us
  waiting for transfers between devices  267 us (45%)
  starting transfers between devices  172 us (29%)
  local copies, waits for them, and re-layouts  89.9 us (15%)
  other arithmetic  35 us (6%)
  matrix products  25.6 us (4%)
    ppermute x8, waiting for transfers between devices, gather_around(): lower.append(lax.ppermute(lower[-1] if lower else x, axis, pairs))  190 us
    ppermute x7, starting transfers between devices, gather_around(): upper.append(lax.ppermute(upper[-1] if upper else x, axis, back))  108 us
    all_to_all x1, waiting for transfers between devices, per_device(): lax.all_to_all(send_b, ('pb', 'ka'), split_axis=1, concat_axis=1, tiled=T...  42.7 us
    ppermute x8, starting transfers between devices, gather_around(): lower.append(lax.ppermute(lower[-1] if lower else x, axis, pairs))  40.5 us
    all_to_all x1, waiting for transfers between devices, per_device(): lax.all_to_all(send_a, ('pb', 'ka'), split_axis=1, concat_axis=1, tiled=T...  30.8 us
    unnamed x61, local copies, waits for them, and re-layouts  26.2 us
    all_to_all x1, starting transfers between devices, per_device(): lax.all_to_all(send_b, ('pb', 'ka'), split_axis=1, concat_axis=1, tiled=T...  20.6 us
    dot_general x24, matrix products, ladder_rows(): product = jnp.dot(left_op, right_op, preferred_element_type=jnp.float32)  17.6 us
  transfers between devices with their start and end apart: 17, of which 12 were waited for; matrix products, arithmetic and copies ran while one was open for 10% of the time, Pallas kernels for 0%

profile of v1, /device:TPU:0, one launch (start us, length us, event | category | flops | bytes accessed | tf_op | source)
XLA Modules:
  0.0 592.1 jit_solution(17407436676142804424)
XLA Ops:
  5.4 27.2 %collective-permute-done = bf16[2,4,64,1024]{3,2,1,0:T(8,128)(2,1)S(1)} collective-permute-done((bf16[2,4,64,1024]{3,2,1,0:T(8,128)(2,1)S(1)}, bf16[2,4,64,1024]{3,2,1,0:T(8,128)(2,1)S(1)}, u32[]{:S(2)}, u32[]{:S(2)}) %collective-permute-start) | collective-permute-done | bytes 1048608 | tf_op jit(solution)/shard_map/ppermute | solution.py:22
  32.6 5.6 collective-permute-start.8
  38.2 39.0 %collective-permute-done.1 = bf16[2,4,64,1024]{3,2,1,0:T(8,128)(2,1)S(1)} collective-permute-done((bf16[2,4,64,1024]{3,2,1,0:T(8,128)(2,1)S(1)}, bf16[2,4,64,1024]{3,2,1,0:T(8,128)(2,1)S(1)}, u32[]{:S(2)}, u32[]{:S(2)}) %collective-permute-start.1) | collective-permute-done | bytes 1048608 | tf_op jit(solution)/shard_map/ppermute | solution.py:22
  80.7 24.3 %collective-permute-start.9 = (bf16[2,4,64,1024]{3,2,1,0:T(8,128)(2,1)S(1)}, bf16[2,4,64,1024]{3,2,1,0:T(8,128)(2,1)S(1)}, u32[]{:S(2)}, u32[]{:S(2)}) collective-permute-start(bf16[2,4,64,1024]{3,2,1,0:T(8,128)(2,1)S(1)} %collective-permute-done.8), channel_id=1, source_target_pairs={{1,0},{2,1},{3,2},{4,3},{5,4},{6,5},{7,6},{8,7},{9,8},{10,9},{11,1... | collective-permute-start | bytes 3145736 | tf_op jit(solution)/shard_map/ppermute | solution.py:24
  105.0 18.4 %collective-permute-done.2 = bf16[2,4,64,1024]{3,2,1,0:T(8,128)(2,1)S(1)} collective-permute-done((bf16[2,4,64,1024]{3,2,1,0:T(8,128)(2,1)S(1)}, bf16[2,4,64,1024]{3,2,1,0:T(8,128)(2,1)S(1)}, u32[]{:S(2)}, u32[]{:S(2)}) %collective-permute-start.2) | collective-permute-done | bytes 1048608 | tf_op jit(solution)/shard_map/ppermute | solution.py:22
  127.6 25.0 %collective-permute-start.10 = (bf16[2,4,64,1024]{3,2,1,0:T(8,128)(2,1)S(1)}, bf16[2,4,64,1024]{3,2,1,0:T(8,128)(2,1)S(1)}, u32[]{:S(2)}, u32[]{:S(2)}) collective-permute-start(bf16[2,4,64,1024]{3,2,1,0:T(8,128)(2,1)S(1)} %collective-permute-done.9), channel_id=1, source_target_pairs={{1,0},{2,1},{3,2},{4,3},{5,4},{6,5},{7,6},{8,7},{9,8},{10,9},{11,1... | collective-permute-start | bytes 3145736 | tf_op jit(solution)/shard_map/ppermute | solution.py:24
  152.6 17.4 %collective-permute-done.3 = bf16[2,4,64,1024]{3,2,1,0:T(8,128)(2,1)S(1)} collective-permute-done((bf16[2,4,64,1024]{3,2,1,0:T(8,128)(2,1)S(1)}, bf16[2,4,64,1024]{3,2,1,0:T(8,128)(2,1)S(1)}, u32[]{:S(2)}, u32[]{:S(2)}) %collective-permute-start.3) | collective-permute-done | bytes 1048608 | tf_op jit(solution)/shard_map/ppermute | solution.py:22
  174.3 25.0 %collective-permute-start.11 = (bf16[2,4,64,1024]{3,2,1,0:T(8,128)(2,1)S(1)}, bf16[2,4,64,1024]{3,2,1,0:T(8,128)(2,1)S(1)}, u32[]{:S(2)}, u32[]{:S(2)}) collective-permute-start(bf16[2,4,64,1024]{3,2,1,0:T(8,128)(2,1)S(1)} %collective-permute-done.10), channel_id=1, source_target_pairs={{1,0},{2,1},{3,2},{4,3},{5,4},{6,5},{7,6},{8,7},{9,8},{10,9},{11,1... | collective-permute-start | bytes 3145736 | tf_op jit(solution)/shard_map/ppermute | solution.py:24
  199.3 16.4 %collective-permute-done.4 = bf16[2,4,64,1024]{3,2,1,0:T(8,128)(2,1)} collective-permute-done((bf16[2,4,64,1024]{3,2,1,0:T(8,128)(2,1)S(1)}, bf16[2,4,64,1024]{3,2,1,0:T(8,128)(2,1)}, u32[]{:S(2)}, u32[]{:S(2)}) %collective-permute-start.4) | collective-permute-done | bytes 1048608 | tf_op jit(solution)/shard_map/ppermute | solution.py:22
  221.1 23.1 %collective-permute-start.12 = (bf16[2,4,64,1024]{3,2,1,0:T(8,128)(2,1)S(1)}, bf16[2,4,64,1024]{3,2,1,0:T(8,128)(2,1)}, u32[]{:S(2)}, u32[]{:S(2)}) collective-permute-start(bf16[2,4,64,1024]{3,2,1,0:T(8,128)(2,1)S(1)} %collective-permute-done.11), channel_id=1, source_target_pairs={{1,0},{2,1},{3,2},{4,3},{5,4},{6,5},{7,6},{8,7},{9,8},{10,9},{11,1... | collective-permute-start | bytes 3145736 | tf_op jit(solution)/shard_map/ppermute | solution.py:24
  244.3 19.1 %collective-permute-done.5 = bf16[2,4,64,1024]{3,2,1,0:T(8,128)(2,1)} collective-permute-done((bf16[2,4,64,1024]{3,2,1,0:T(8,128)(2,1)}, bf16[2,4,64,1024]{3,2,1,0:T(8,128)(2,1)}, u32[]{:S(2)}, u32[]{:S(2)}) %collective-permute-start.5) | collective-permute-done | bytes 1048608 | tf_op jit(solution)/shard_map/ppermute | solution.py:22
  263.4 25.0 %collective-permute-start.6 = (bf16[2,4,64,1024]{3,2,1,0:T(8,128)(2,1)}, bf16[2,4,64,1024]{3,2,1,0:T(8,128)(2,1)}, u32[]{:S(2)}, u32[]{:S(2)}) collective-permute-start(bf16[2,4,64,1024]{3,2,1,0:T(8,128)(2,1)} %collective-permute-done.5), channel_id=1, source_target_pairs={{0,1},{1,2},{2,3},{3,4},{4,5},{5,6},{6,7},{7,8},{8,9},{9,10},{10,1... | collective-permute-start | bytes 3145736 | tf_op jit(solution)/shard_map/ppermute | solution.py:22
  291.9 39.8 %collective-permute-done.6 = bf16[2,4,64,1024]{3,2,1,0:T(8,128)(2,1)} collective-permute-done((bf16[2,4,64,1024]{3,2,1,0:T(8,128)(2,1)}, bf16[2,4,64,1024]{3,2,1,0:T(8,128)(2,1)}, u32[]{:S(2)}, u32[]{:S(2)}) %collective-permute-start.6) | collective-permute-done | bytes 1048608 | tf_op jit(solution)/shard_map/ppermute | solution.py:22
  340.0 13.1 %collective-permute-done.7 = bf16[2,4,64,1024]{3,2,1,0:T(8,128)(2,1)} collective-permute-done((bf16[2,4,64,1024]{3,2,1,0:T(8,128)(2,1)}, bf16[2,4,64,1024]{3,2,1,0:T(8,128)(2,1)}, u32[]{:S(2)}, u32[]{:S(2)}) %collective-permute-start.7) | collective-permute-done | bytes 1048608 | tf_op jit(solution)/shard_map/ppermute | solution.py:22
  378.3 13.4 %gather_fusion = bf16[16,2,4,64,1024]{4,3,2,1,0:T(8,128)(2,1)} fusion(bf16[16,2,4,64,1024]{4,3,2,1,0:T(8,128)(2,1)} %bitcast_dynamic-update-slice_fusion, s32[1024]{0:T(1024)S(1)} %pad_clamp_fusion.5), kind=kCustom, calls=%fused_computation.4 | custom fusion | bytes 33554496 | tf_op jit(solution)/shard_map/gather | solution.py:27
  391.7 14.1 %copy.36 = bf16[2,4,16,64,1024]{4,3,2,0,1:T(8,128)(2,1)} copy(bf16[2,4,16,64,1024]{4,3,1,0,2:T(8,128)(2,1)} %bitcast.324) | data formatting | bytes 33554432 | tf_op jit(solution)/shard_map/transpose | solution.py:12
  405.7 37.3 %while.10 = (s32[]{:T(128)}, f32[4,2,64,1024]{3,2,0,1:T(8,128)}, f32[4,2,64,1024]{3,2,1,0:T(8,128)S(1)}, f32[4,2,1024]{2,1,0:T(2,128)S(1)}, bf16[4,2,1024,1024]{...) while((s32[]{:T(128)}, f32[4,2,64,1024]{3,2,0,1:T(8,128)}, f32[4,2,64,1024]{3,2,1,0:T(8,128)S(1)}, ...), condition=%wide.region_1.2_spmd, body=%wide.region_0.1_spmd.sunk | while | flops 3280207872 | bytes 65077900 | solution.py:58
  447.3 4.0 gather_fusion.5
  454.9 20.6 %all-to-all-start.1 = ((f32[2,256,1024]{2,0,1:T(2,128)}), f32[2,256,1024]{2,0,1:T(2,128)}, u32[]{:S(2)}, u32[]{:S(2)}) async-start(f32[2,256,1024]{2,0,1:T(2,128)} %select_bitcast_fusion.1), calls=%async_computation.1 | async-start | bytes 4194304 | tf_op jit(solution)/shard_map/all_to_all | solution.py:118
  475.6 4.0 gather_fusion.3
  483.2 42.7 %all-to-all-done.1 = f32[2,256,1024]{2,0,1:T(2,128)} async-done(((f32[2,256,1024]{2,0,1:T(2,128)}), f32[2,256,1024]{2,0,1:T(2,128)}, u32[]{:S(2)}, u32[]{:S(2)}) %all-to-all-start.1) | async-done | bytes 2097184 | tf_op jit(solution)/shard_map/all_to_all | solution.py:118
  534.4 5.6 gather_fusion.6
  548.4 30.8 %all-to-all-done = f32[2,256,1024]{2,0,1:T(2,128)S(1)} async-done(((f32[2,256,1024]{2,0,1:T(2,128)}), f32[2,256,1024]{2,0,1:T(2,128)S(1)}, u32[]{:S(2)}, u32[]{:S(2)}) %all-to-all-start) | async-done | bytes 2097184 | tf_op jit(solution)/shard_map/all_to_all | solution.py:117
  579.2 4.0 gather_fusion.4
  (261 shorter events, 132.6 us)
Async XLA Ops:
  0.6 217.6 %copy-start.19 = (s32[2,8,1024]{2,1,0:T(8,128)S(1)}, s32[2,8,1024]{2,1,0:T(8,128)}, u32[]{:S(2)}) copy-start(s32[2,8,1024]{2,1,0:T(8,128)} %param.14) | copy-start | bytes 196612
  2.4 30.2 %collective-permute-start = (bf16[2,4,64,1024]{3,2,1,0:T(8,128)(2,1)S(1)}, bf16[2,4,64,1024]{3,2,1,0:T(8,128)(2,1)S(1)}, u32[]{:S(2)}, u32[]{:S(2)}) collective-permute-start(bf16[2,4,64,1024]{3,2,1,0:T(8,128)(2,1)S(1)} %convert_element_type.47), channel_id=1, source_target_pairs={{0,1},{1,2},{2,3},{3,4},{4,5},{5,6},{6,7},{7,8},{8,9},{9,10},{10,1... | collective-permute-start | bytes 3145736 | tf_op jit(solution)/shard_map/ppermute | solution.py:22
  32.6 44.6 %collective-permute-start.1 = (bf16[2,4,64,1024]{3,2,1,0:T(8,128)(2,1)S(1)}, bf16[2,4,64,1024]{3,2,1,0:T(8,128)(2,1)S(1)}, u32[]{:S(2)}, u32[]{:S(2)}) collective-permute-start(bf16[2,4,64,1024]{3,2,1,0:T(8,128)(2,1)S(1)} %collective-permute-done), channel_id=1, source_target_pairs={{0,1},{1,2},{2,3},{3,4},{4,5},{5,6},{6,7},{7,8},{8,9},{9,10},{10,1... | collective-permute-start | bytes 3145736 | tf_op jit(solution)/shard_map/ppermute | solution.py:22
  32.6 47.1 %collective-permute-start.8 = (bf16[2,4,64,1024]{3,2,1,0:T(8,128)(2,1)S(1)}, bf16[2,4,64,1024]{3,2,1,0:T(8,128)(2,1)S(1)}, u32[]{:S(2)}, u32[]{:S(2)}) collective-permute-start(bf16[2,4,64,1024]{3,2,1,0:T(8,128)(2,1)S(1)} %convert_element_type.47), channel_id=1, source_target_pairs={{1,0},{2,1},{3,2},{4,3},{5,4},{6,5},{7,6},{8,7},{9,8},{10,9},{11,1... | collective-permute-start | bytes 3145736 | tf_op jit(solution)/shard_map/ppermute | solution.py:24
  77.2 50.4 %copy-start.5 = (bf16[2,4,64,1024]{3,2,1,0:T(8,128)(2,1)}, bf16[2,4,64,1024]{3,2,1,0:T(8,128)(2,1)S(1)}, u32[]{:S(2)}) copy-start(bf16[2,4,64,1024]{3,2,1,0:T(8,128)(2,1)S(1)} %collective-permute-done.1) | copy-start | bytes 3145732
  77.2 46.2 %collective-permute-start.2 = (bf16[2,4,64,1024]{3,2,1,0:T(8,128)(2,1)S(1)}, bf16[2,4,64,1024]{3,2,1,0:T(8,128)(2,1)S(1)}, u32[]{:S(2)}, u32[]{:S(2)}) collective-permute-start(bf16[2,4,64,1024]{3,2,1,0:T(8,128)(2,1)S(1)} %collective-permute-done.1), channel_id=1, source_target_pairs={{0,1},{1,2},{2,3},{3,4},{4,5},{5,6},{6,7},{7,8},{8,9},{9,10},{10,1... | collective-permute-start | bytes 3145736 | tf_op jit(solution)/shard_map/ppermute | solution.py:22
  80.7 46.9 %collective-permute-start.9 = (bf16[2,4,64,1024]{3,2,1,0:T(8,128)(2,1)S(1)}, bf16[2,4,64,1024]{3,2,1,0:T(8,128)(2,1)S(1)}, u32[]{:S(2)}, u32[]{:S(2)}) collective-permute-start(bf16[2,4,64,1024]{3,2,1,0:T(8,128)(2,1)S(1)} %collective-permute-done.8), channel_id=1, source_target_pairs={{1,0},{2,1},{3,2},{4,3},{5,4},{6,5},{7,6},{8,7},{9,8},{10,9},{11,1... | collective-permute-start | bytes 3145736 | tf_op jit(solution)/shard_map/ppermute | solution.py:24
  123.4 50.9 %copy-start.9 = (bf16[2,4,64,1024]{3,2,1,0:T(8,128)(2,1)}, bf16[2,4,64,1024]{3,2,1,0:T(8,128)(2,1)S(1)}, u32[]{:S(2)}) copy-start(bf16[2,4,64,1024]{3,2,1,0:T(8,128)(2,1)S(1)} %collective-permute-done.2) | copy-start | bytes 3145732
  123.4 46.6 %collective-permute-start.3 = (bf16[2,4,64,1024]{3,2,1,0:T(8,128)(2,1)S(1)}, bf16[2,4,64,1024]{3,2,1,0:T(8,128)(2,1)S(1)}, u32[]{:S(2)}, u32[]{:S(2)}) collective-permute-start(bf16[2,4,64,1024]{3,2,1,0:T(8,128)(2,1)S(1)} %collective-permute-done.2), channel_id=1, source_target_pairs={{0,1},{1,2},{2,3},{3,4},{4,5},{5,6},{6,7},{7,8},{8,9},{9,10},{10,1... | collective-permute-start | bytes 3145736 | tf_op jit(solution)/shard_map/ppermute | solution.py:22
  127.6 46.7 %collective-permute-start.10 = (bf16[2,4,64,1024]{3,2,1,0:T(8,128)(2,1)S(1)}, bf16[2,4,64,1024]{3,2,1,0:T(8,128)(2,1)S(1)}, u32[]{:S(2)}, u32[]{:S(2)}) collective-permute-start(bf16[2,4,64,1024]{3,2,1,0:T(8,128)(2,1)S(1)} %collective-permute-done.9), channel_id=1, source_target_pairs={{1,0},{2,1},{3,2},{4,3},{5,4},{6,5},{7,6},{8,7},{9,8},{10,9},{11,1... | collective-permute-start | bytes 3145736 | tf_op jit(solution)/shard_map/ppermute | solution.py:24
  170.0 45.6 %collective-permute-start.4 = (bf16[2,4,64,1024]{3,2,1,0:T(8,128)(2,1)S(1)}, bf16[2,4,64,1024]{3,2,1,0:T(8,128)(2,1)}, u32[]{:S(2)}, u32[]{:S(2)}) collective-permute-start(bf16[2,4,64,1024]{3,2,1,0:T(8,128)(2,1)S(1)} %collective-permute-done.3), channel_id=1, source_target_pairs={{0,1},{1,2},{2,3},{3,4},{4,5},{5,6},{6,7},{7,8},{8,9},{9,10},{10,1... | collective-permute-start | bytes 3145736 | tf_op jit(solution)/shard_map/ppermute | solution.py:22
  174.3 159.8 %copy-start.11 = (bf16[2,4,64,1024]{3,2,1,0:T(8,128)(2,1)}, bf16[2,4,64,1024]{3,2,1,0:T(8,128)(2,1)S(1)}, u32[]{:S(2)}) copy-start(bf16[2,4,64,1024]{3,2,1,0:T(8,128)(2,1)S(1)} %collective-permute-done.10) | copy-start | bytes 3145732
  174.3 46.8 %collective-permute-start.11 = (bf16[2,4,64,1024]{3,2,1,0:T(8,128)(2,1)S(1)}, bf16[2,4,64,1024]{3,2,1,0:T(8,128)(2,1)S(1)}, u32[]{:S(2)}, u32[]{:S(2)}) collective-permute-start(bf16[2,4,64,1024]{3,2,1,0:T(8,128)(2,1)S(1)} %collective-permute-done.10), channel_id=1, source_target_pairs={{1,0},{2,1},{3,2},{4,3},{5,4},{6,5},{7,6},{8,7},{9,8},{10,9},{11,1... | collective-permute-start | bytes 3145736 | tf_op jit(solution)/shard_map/ppermute | solution.py:24
  215.6 47.7 %collective-permute-start.5 = (bf16[2,4,64,1024]{3,2,1,0:T(8,128)(2,1)}, bf16[2,4,64,1024]{3,2,1,0:T(8,128)(2,1)}, u32[]{:S(2)}, u32[]{:S(2)}) collective-permute-start(bf16[2,4,64,1024]{3,2,1,0:T(8,128)(2,1)} %collective-permute-done.4), channel_id=1, source_target_pairs={{0,1},{1,2},{2,3},{3,4},{4,5},{5,6},{6,7},{7,8},{8,9},{9,10},{10,1... | collective-permute-start | bytes 3145736 | tf_op jit(solution)/shard_map/ppermute | solution.py:22
  221.1 113.0 %copy-start.13 = (bf16[2,4,64,1024]{3,2,1,0:T(8,128)(2,1)}, bf16[2,4,64,1024]{3,2,1,0:T(8,128)(2,1)S(1)}, u32[]{:S(2)}) copy-start(bf16[2,4,64,1024]{3,2,1,0:T(8,128)(2,1)S(1)} %collective-permute-done.11) | copy-start | bytes 3145732
  221.1 68.5 %collective-permute-start.12 = (bf16[2,4,64,1024]{3,2,1,0:T(8,128)(2,1)S(1)}, bf16[2,4,64,1024]{3,2,1,0:T(8,128)(2,1)}, u32[]{:S(2)}, u32[]{:S(2)}) collective-permute-start(bf16[2,4,64,1024]{3,2,1,0:T(8,128)(2,1)S(1)} %collective-permute-done.11), channel_id=1, source_target_pairs={{1,0},{2,1},{3,2},{4,3},{5,4},{6,5},{7,6},{8,7},{9,8},{10,9},{11,1... | collective-permute-start | bytes 3145736 | tf_op jit(solution)/shard_map/ppermute | solution.py:24
  263.4 68.3 %collective-permute-start.6 = (bf16[2,4,64,1024]{3,2,1,0:T(8,128)(2,1)}, bf16[2,4,64,1024]{3,2,1,0:T(8,128)(2,1)}, u32[]{:S(2)}, u32[]{:S(2)}) collective-permute-start(bf16[2,4,64,1024]{3,2,1,0:T(8,128)(2,1)} %collective-permute-done.5), channel_id=1, source_target_pairs={{0,1},{1,2},{2,3},{3,4},{4,5},{5,6},{6,7},{7,8},{8,9},{9,10},{10,1... | collective-permute-start | bytes 3145736 | tf_op jit(solution)/shard_map/ppermute | solution.py:22
  289.7 47.2 %collective-permute-start.13 = (bf16[2,4,64,1024]{3,2,1,0:T(8,128)(2,1)}, bf16[2,4,64,1024]{3,2,1,0:T(8,128)(2,1)}, u32[]{:S(2)}, u32[]{:S(2)}) collective-permute-start(bf16[2,4,64,1024]{3,2,1,0:T(8,128)(2,1)} %collective-permute-done.12), channel_id=1, source_target_pairs={{1,0},{2,1},{3,2},{4,3},{5,4},{6,5},{7,6},{8,7},{9,8},{10,9},{11,1... | collective-permute-start | bytes 3145736 | tf_op jit(solution)/shard_map/ppermute | solution.py:24
  331.7 21.5 %collective-permute-start.7 = (bf16[2,4,64,1024]{3,2,1,0:T(8,128)(2,1)}, bf16[2,4,64,1024]{3,2,1,0:T(8,128)(2,1)}, u32[]{:S(2)}, u32[]{:S(2)}) collective-permute-start(bf16[2,4,64,1024]{3,2,1,0:T(8,128)(2,1)} %collective-permute-done.6), channel_id=1, source_target_pairs={{0,1},{1,2},{2,3},{3,4},{4,5},{5,6},{6,7},{7,8},{8,9},{9,10},{10,1... | collective-permute-start | bytes 3145736 | tf_op jit(solution)/shard_map/ppermute | solution.py:22
  336.8 40.3 %collective-permute-start.14 = (bf16[2,4,64,1024]{3,2,1,0:T(8,128)(2,1)}, bf16[2,4,64,1024]{3,2,1,0:T(8,128)(2,1)S(1)}, u32[]{:S(2)}, u32[]{:S(2)}) collective-permute-start(bf16[2,4,64,1024]{3,2,1,0:T(8,128)(2,1)} %collective-permute-done.13), channel_id=1, source_target_pairs={{1,0},{2,1},{3,2},{4,3},{5,4},{6,5},{7,6},{8,7},{9,8},{10,9},{11,1... | collective-permute-start | bytes 3145736 | tf_op jit(solution)/shard_map/ppermute | solution.py:24
  454.9 71.0 %all-to-all-start.1 = ((f32[2,256,1024]{2,0,1:T(2,128)}), f32[2,256,1024]{2,0,1:T(2,128)}, u32[]{:S(2)}, u32[]{:S(2)}) async-start(f32[2,256,1024]{2,0,1:T(2,128)} %select_bitcast_fusion.1), calls=%async_computation.1 | async-start | bytes 4194304 | tf_op jit(solution)/shard_map/all_to_all | solution.py:118
  483.2 45.6 %copy-start.17 = (s32[1,8,8,128]{3,2,1,0:T(8,128)S(1)}, s32[1,8,8,128]{3,2,1,0:T(8,128)}, u32[]{:S(2)}) copy-start(s32[1,8,8,128]{3,2,1,0:T(8,128)} %get-tuple-element.74) | copy-start | bytes 98308
  483.2 45.6 %copy-start.18 = (s32[1,8,8,128]{3,2,1,0:T(8,128)S(1)}, s32[1,8,8,128]{3,2,1,0:T(8,128)}, u32[]{:S(2)}) copy-start(s32[1,8,8,128]{3,2,1,0:T(8,128)} %get-tuple-element.75) | copy-start | bytes 98308
  525.9 53.3 %all-to-all-start = ((f32[2,256,1024]{2,0,1:T(2,128)}), f32[2,256,1024]{2,0,1:T(2,128)S(1)}, u32[]{:S(2)}, u32[]{:S(2)}) async-start(f32[2,256,1024]{2,0,1:T(2,128)} %select_bitcast_fusion.3), calls=%async_computation | async-start | bytes 4194304 | tf_op jit(solution)/shard_map/all_to_all | solution.py:117
  (15 other events, 92.7 us)
